TPU v7x, 256 devices: a whole 4x4x8 slice. The times are simulated.
256 devices in a mesh: shard: 64 (over z, x_lo, y), blk: 4 (over x_hi, core).
Axes of the slice: x: 4 (x_hi: 2, x_lo: 2; x = x_hi * 2 + x_lo), y: 4, z: 8, core: 2. Of those that a mesh axis runs over, the one named last changes fastest.
Arguments:
- embeddings: bfloat16 [65536, 1024], P(('shard', 'blk')), may hold values from -6 to 6
- doc_cluster: int32 [65536], P(('shard', 'blk')), may hold values from 0 to 255, as said below
- doc_valid: int32 [65536], P(('shard', 'blk')), may hold values 0 or 1
Outputs:
- max_similar: float32 [65536], P(('shard', 'blk'))
Inputs may be any that keep to these rules, and one draw needn't show every extreme that they name: `doc_cluster`: among the documents of one device at most 16 have clusters of one owner group (cluster mod 64), and at most 4 have clusters c of one owner group with one value of (c // 64) mod 4; one owner group, the same on every device, gets exactly 16 from every device, 4 for each such value.
All inputs are finite; a program needn't handle non-finite values. No bound on the sum of `doc_valid` on one device may be relied on, other than what follows from the above.
Results may differ from a plain program's by a relative error of at most 0.00036.
Values may be sent and summed in bfloat16 or wider, within the bound.
A program may use at most 64 MiB of HBM per device.

v0:
```python
import math

import jax
import jax.numpy as jnp
from jax import lax
from jax.sharding import PartitionSpec as P


def unit_rows(embeddings):
    values = embeddings.astype(jnp.float32)
    scale = lax.rsqrt(jnp.mean(values * values, axis=1, keepdims=True) + 1e-05) / math.sqrt(
        values.shape[1]
    )
    return (values * scale).astype(jnp.bfloat16)


def scores_max(rows_query, keys_query, ids_query, rows_other, keys_other, ids_other, key_block):
    query_count = rows_query.shape[0]
    block_rows = 512

    def one_block(block):
        rows_part, keys_part, ids_part = block
        best = jnp.full((rows_part.shape[0],), -1.0, jnp.float32)
        for number in range(rows_other.shape[0] // key_block):
            first = number * key_block
            rows_key = rows_other[first : first + key_block]
            keys_key = keys_other[first : first + key_block]
            ids_key = ids_other[first : first + key_block]
            similar = lax.dot_general(
                rows_part, rows_key, (((1,), (1,)), ((), ())), preferred_element_type=jnp.float32
            )
            same_group = (
                (keys_part[:, None] == keys_key[None, :])
                & (keys_part[:, None] >= 0)
                & (ids_part[:, None] != ids_key[None, :])
            )
            best = jnp.maximum(best, jnp.max(jnp.where(same_group, similar, -1.0), axis=1))
        return best

    stacked = (
        rows_query.reshape(query_count // block_rows, block_rows, -1),
        keys_query.reshape(query_count // block_rows, block_rows),
        ids_query.reshape(query_count // block_rows, block_rows),
    )
    return lax.map(one_block, stacked).reshape(query_count)


def slot_numbers(target, targets, per_target):
    one_hot = (target[:, None] == jnp.arange(targets, dtype=jnp.int32)[None, :]).astype(jnp.int32)
    ranks = jnp.sum((jnp.cumsum(one_hot, axis=0) - 1) * one_hot, axis=1)
    return target * per_target + ranks


def per_device(embeddings, doc_cluster, doc_valid):
    dev_rows, width = embeddings.shape
    shards = lax.axis_size("shard")
    blocks = lax.axis_size("blk")
    capacity = max(blocks, 4 * dev_rows // shards)
    slots = shards * capacity
    device = lax.axis_index("shard") * blocks + lax.axis_index("blk")
    doc_ids = device * dev_rows + jnp.arange(dev_rows, dtype=jnp.int32)
    owner = doc_cluster % shards
    slot_of = slot_numbers(owner, shards, capacity)
    keyed = jnp.where(doc_valid > 0, doc_cluster, -1)
    flat_rows = jnp.zeros((slots, width), jnp.bfloat16).at[slot_of].set(unit_rows(embeddings))
    flat_keys = jnp.full((slots,), -1, jnp.int32).at[slot_of].set(keyed)
    flat_ids = jnp.full((slots,), -1, jnp.int32).at[slot_of].set(doc_ids)
    send_rows = flat_rows.reshape(shards, capacity, width)
    send_keys = flat_keys.reshape(shards, capacity)
    send_ids = flat_ids.reshape(shards, capacity)
    got_rows, got_keys, got_ids = (
        lax.all_to_all(send_rows, "shard", split_axis=0, concat_axis=0, tiled=True),
        lax.all_to_all(send_keys, "shard", split_axis=0, concat_axis=0, tiled=True),
        lax.all_to_all(send_ids, "shard", split_axis=0, concat_axis=0, tiled=True),
    )
    query_rows = got_rows.reshape(slots, width)
    query_keys = got_keys.reshape(slots)
    query_ids = got_ids.reshape(slots)
    best = jnp.maximum(
        jnp.full((slots,), -1.0, jnp.float32),
        scores_max(
            query_rows,
            query_keys,
            query_ids,
            lax.all_gather(query_rows, "blk", axis=0, tiled=True),
            lax.all_gather(query_keys, "blk", axis=0, tiled=True),
            lax.all_gather(query_ids, "blk", axis=0, tiled=True),
            slots,
        ),
    )
    verdict = lax.all_to_all(
        best.reshape(shards, capacity), "shard", split_axis=0, concat_axis=0, tiled=True
    )
    return verdict.reshape(slots)[slot_of]


def solution(mesh):
    placed = (P(("shard", "blk"), None), P(("shard", "blk")), P(("shard", "blk")))
    return jax.shard_map(
        per_device, mesh=mesh, in_specs=placed, out_specs=P(("shard", "blk")), check_vma=False
    )
```

profile of v0, /device:TPU:1, one launch (start us, length us, event | category | flops | bytes accessed | tf_op | source)
XLA Modules:
  0.0 188.0 jit_solution(3267887966830044788)
XLA Ops:
  6.5 0.0 all-gather.2.cloned.1.call-start
  6.5 0.7 compare_select_fusion.3
  7.3 0.6 reduce-window.6
  7.9 0.2 slice_reduce_fusion
  8.1 0.1 fusion.35
  8.2 1.2 fusion.28
  9.5 2.9 %scatter_custom_fusion.2 = bf16[1024,1024]{1,0:T(8,128)(2,1)S(1)} fusion(s32[256]{0:T(256)S(1)} %get-tuple-element.80, bf16[]{:T(256)} %constant.32.clone.1, bf16[256,1024]{1,0:T(8,128)(2,1)} %param.5, f32[256]{0:T(256)S(1)} %rsqrt_multiply_fusion), kind=kCustom, calls=%fused_computation.36 | custom fusion | flops 786432 | bytes 2622466 | tf_op jit(solution)/shard_map/scatter | solution.py:65
  12.4 61.9 %all_to_all.29 = bf16[64,16,1024]{2,1,0:T(8,128)(2,1)} all-to-all(bf16[64,16,1024]{2,1,0:T(8,128)(2,1)S(1)} %bitcast.52), channel_id=1, replica_groups=mesh['shard'=64,'blk'=4] {'shard'}, dimensions={0} | all-to-all | bytes 4194304 | tf_op jit(solution)/shard_map/all_to_all | solution.py:72
  74.3 0.0 all-gather.2.cloned.1.call-update
  74.3 1.4 scatter_custom_fusion.1
  75.7 0.7 all_to_all.21
  76.4 7.6 %all-to-all-start.1 = ((s32[64,1,16]{2,1,0:T(1,128)}), s32[64,1,16]{2,1,0:T(1,128)S(1)}, u32[]{:S(2)}, u32[]{:S(2)}) async-start(s32[64,1,16]{2,1,0:T(1,128)} %bitcast.7), calls=%async_computation.1 | async-start | bytes 65536 | tf_op jit(solution)/shard_map/all_to_all | solution.py:74
  84.1 1.4 scatter_custom_fusion
  85.5 0.7 all_to_all.19
  86.2 7.2 %all-to-all-done.1 = s32[64,1,16]{2,1,0:T(1,128)S(1)} async-done(((s32[64,1,16]{2,1,0:T(1,128)}), s32[64,1,16]{2,1,0:T(1,128)S(1)}, u32[]{:S(2)}, u32[]{:S(2)}) %all-to-all-start.1) | async-done | bytes 4128 | tf_op jit(solution)/shard_map/all_to_all | solution.py:74
  93.4 4.6 %all-to-all-start = ((s32[64,1,16]{2,1,0:T(1,128)}), s32[64,1,16]{2,1,0:T(1,128)S(1)}, u32[]{:S(2)}, u32[]{:S(2)}) async-start(s32[64,1,16]{2,1,0:T(1,128)} %bitcast.6), calls=%async_computation | async-start | bytes 65536 | tf_op jit(solution)/shard_map/all_to_all | solution.py:73
  98.0 0.6 broadcast.127
  98.5 0.7 reduce.16
  99.3 0.1 reshape_reshape.10
  99.4 0.1 reshape.127
  99.5 7.8 %all-to-all-done = s32[64,1,16]{2,1,0:T(1,128)S(1)} async-done(((s32[64,1,16]{2,1,0:T(1,128)}), s32[64,1,16]{2,1,0:T(1,128)S(1)}, u32[]{:S(2)}, u32[]{:S(2)}) %all-to-all-start) | async-done | bytes 4128 | tf_op jit(solution)/shard_map/all_to_all | solution.py:73
  107.2 0.7 reduce.15
  108.0 0.1 reshape_reshape.9
  108.1 0.1 reshape.126
  108.1 10.9 %all_gather.10 = s32[4096]{0:T(1024)S(1)} all-gather(s32[1024]{0:T(1024)S(1)} %reshape.127), channel_id=1, replica_groups=mesh['shard'=64,'blk'=4] {'blk'}, dimensions={0}, use_global_device_ids=true | all-gather | bytes 20480 | tf_op jit(solution)/shard_map/all_gather | solution.py:87
  119.0 6.9 %all_gather.9 = s32[4096]{0:T(1024)S(1)} all-gather(s32[1024]{0:T(1024)S(1)} %reshape.126), channel_id=1, replica_groups=mesh['shard'=64,'blk'=4] {'blk'}, dimensions={0}, use_global_device_ids=true | all-gather | bytes 20480 | tf_op jit(solution)/shard_map/all_gather | solution.py:86
  125.9 14.1 %all-gather.2.cloned.1.call-done = bf16[4096,1024]{1,0:T(8,128)(2,1)} async-done(((bf16[1024,1024]{1,0:T(8,128)(2,1)}), bf16[4096,1024]{1,0:T(8,128)(2,1)}) %all-gather.2.cloned.1.call-update) | async-done | bytes 8388624 | tf_op jit(solution)/shard_map/all_gather | solution.py:85
  140.0 0.0 copy-done
  140.1 17.7 %while.10 = (s32[]{:T(128)}, f32[2,512]{1,0:T(2,128)S(1)}, s32[2,512]{1,0:T(2,128)S(1)}, s32[4096]{0:T(1024)S(1)}, s32[2,512]{1,0:T(2,128)S(1)}, /*index=5*/s32[...) while((s32[]{:T(128)}, f32[2,512]{1,0:T(2,128)S(1)}, ...), condition=%wide.region_12.13_spmd, body=%wide.region_7.12_spmd.sunk | while | flops 4307550720 | bytes 46288020 | solution.py:45
  140.1 0.0 copy-start.1
  140.1 3.3 %select_reduce_fusion.11 = f32[512]{0:T(512)S(1)} fusion(bf16[4096,1024]{1,0:T(8,128)(2,1)} %get-tuple-element.178, s32[1024]{0:T(1024)S(1)} %get-tuple-element.149, s32[1024]{0:T(1024)S(1)} %get-tuple-element.150, pred[512]{0:T(512)(128)(4,1)S(1)} %broadcast_compare_fusion.2, s32[512]{0:T(512)S(1)} %bitcast.61, s32[512]{0:T(512)S(1)} %bitcast.56, ...), kind=kOutput, calls=%fused_computation.13.clone.1 | convolution fusion | flops 1076887040 | bytes 3161088 | tf_op jit(solution)/shard_map/while/body/eval_jaxpr/dot_general | solution.py:29
  143.4 0.7 copy-done.1
  144.1 1.6 select_reduce_fusion.10
  145.7 1.6 select_reduce_fusion.9
  147.3 1.6 select_reduce_fusion.8
  149.0 0.0 copy-start.1
  149.0 3.3 %select_reduce_fusion.11 = f32[512]{0:T(512)S(1)} fusion(bf16[4096,1024]{1,0:T(8,128)(2,1)} %get-tuple-element.178, s32[1024]{0:T(1024)S(1)} %get-tuple-element.149, s32[1024]{0:T(1024)S(1)} %get-tuple-element.150, pred[512]{0:T(512)(128)(4,1)S(1)} %broadcast_compare_fusion.2, s32[512]{0:T(512)S(1)} %bitcast.61, s32[512]{0:T(512)S(1)} %bitcast.56, ...), kind=kOutput, calls=%fused_computation.13.clone.1 | convolution fusion | flops 1076887040 | bytes 3161088 | tf_op jit(solution)/shard_map/while/body/eval_jaxpr/dot_general | solution.py:29
  152.3 0.7 copy-done.1
  153.0 1.6 select_reduce_fusion.10
  154.6 1.6 select_reduce_fusion.9
  156.1 1.6 select_reduce_fusion.8
  157.8 0.7 max_broadcast_in_dim.15
  158.5 10.1 %all-to-all-start.3 = ((f32[64,1,16]{2,1,0:T(1,128)}), f32[64,1,16]{2,1,0:T(1,128)S(1)}, u32[]{:S(2)}, u32[]{:S(2)}) async-start(f32[64,1,16]{2,1,0:T(1,128)} %bitcast.11), calls=%async_computation.3 | async-start | bytes 65536 | tf_op jit(solution)/shard_map/all_to_all | solution.py:91
  168.6 9.3 %all-to-all-done.3 = f32[64,1,16]{2,1,0:T(1,128)S(1)} async-done(((f32[64,1,16]{2,1,0:T(1,128)}), f32[64,1,16]{2,1,0:T(1,128)S(1)}, u32[]{:S(2)}, u32[]{:S(2)}) %all-to-all-start.3) | async-done | bytes 4128 | tf_op jit(solution)/shard_map/all_to_all | solution.py:91
  177.9 0.5 broadcast.129
  178.4 0.7 reduce.17
  179.2 0.1 reshape.130
  179.3 1.9 %gather_fusion = f32[256]{0:T(256)} fusion(f32[1024]{0:T(1024)S(1)} %reshape.130, s32[1024]{0:T(1024)S(1)} %pad_clamp_fusion), kind=kCustom, calls=%fused_computation | custom fusion | bytes 3072 | tf_op jit(solution)/shard_map/gather | solution.py:94
  (19 shorter events, 0.2 us)
Async XLA Ops:
  6.5 133.5 %all-gather.2.cloned.1.call-start = ((), (), s32[]{:S(2)}) async-start(), calls=%async_computation.4 | async-start | bytes 10485760 | tf_op jit(solution)/shard_map/all_gather | solution.py:85
  74.3 65.7 %copy-start = (bf16[64,16,1024]{2,1,0:T(8,128)(2,1)S(1)}, bf16[64,16,1024]{2,1,0:T(8,128)(2,1)}, u32[]{:S(2)}) copy-start(bf16[64,16,1024]{2,1,0:T(8,128)(2,1)} %all_to_all.29) | copy-start | bytes 6291460
  76.4 16.9 %all-to-all-start.1 = ((s32[64,1,16]{2,1,0:T(1,128)}), s32[64,1,16]{2,1,0:T(1,128)S(1)}, u32[]{:S(2)}, u32[]{:S(2)}) async-start(s32[64,1,16]{2,1,0:T(1,128)} %bitcast.7), calls=%async_computation.1 | async-start | bytes 65536 | tf_op jit(solution)/shard_map/all_to_all | solution.py:74
  93.4 13.9 %all-to-all-start = ((s32[64,1,16]{2,1,0:T(1,128)}), s32[64,1,16]{2,1,0:T(1,128)S(1)}, u32[]{:S(2)}, u32[]{:S(2)}) async-start(s32[64,1,16]{2,1,0:T(1,128)} %bitcast.6), calls=%async_computation | async-start | bytes 65536 | tf_op jit(solution)/shard_map/all_to_all | solution.py:73
  140.1 4.0 %copy-start.1 = (bf16[4096,1024]{1,0:T(8,128)(2,1)S(1)}, bf16[4096,1024]{1,0:T(8,128)(2,1)}, u32[]{:S(2)}) copy-start(bf16[4096,1024]{1,0:T(8,128)(2,1)} %get-tuple-element.178) | copy-start | bytes 25165828 | tf_op jit(solution)/shard_map/while
  149.0 4.0 %copy-start.1 = (bf16[4096,1024]{1,0:T(8,128)(2,1)S(1)}, bf16[4096,1024]{1,0:T(8,128)(2,1)}, u32[]{:S(2)}) copy-start(bf16[4096,1024]{1,0:T(8,128)(2,1)} %get-tuple-element.178) | copy-start | bytes 25165828 | tf_op jit(solution)/shard_map/while
  158.5 19.5 %all-to-all-start.3 = ((f32[64,1,16]{2,1,0:T(1,128)}), f32[64,1,16]{2,1,0:T(1,128)S(1)}, u32[]{:S(2)}, u32[]{:S(2)}) async-start(f32[64,1,16]{2,1,0:T(1,128)} %bitcast.11), calls=%async_computation.3 | async-start | bytes 65536 | tf_op jit(solution)/shard_map/all_to_all | solution.py:91
Sparse Core Ops, SparseCore 0:
  74.5 65.5 all-gather.1
where the time goes:
time: 188 us
  blocking collectives  79.7 us (42%)
  waiting for transfers between devices  38.4 us (20%)
  starting transfers between devices  22.3 us (12%)
  matrix products  16.1 us (9%)
  between operations  13.5 us (7%)
  local copies, waits for them, and re-layouts  9.96 us (5%)
  other arithmetic  7.88 us (4%)
    all_to_all x1, blocking collectives, per_device(): lax.all_to_all(send_rows, 'shard', split_axis=0, concat_axis=0, tiled=True)  61.9 us
    dot_general x8, matrix products, one_block(): lax.dot_general(rows_part, rows_key, (((1,), (1,)), ((), ())), preferred_...  16.1 us
    all_gather x1, waiting for transfers between devices, per_device(): lax.all_gather(query_rows, 'blk', axis=0, tiled=True)  14.1 us
    all_gather x1, blocking collectives, per_device(): lax.all_gather(query_ids, 'blk', axis=0, tiled=True)  10.9 us
    all_to_all x1, starting transfers between devices, per_device(): lax.all_to_all(best.reshape(shards, capacity), 'shard', split_axis=0, con...  10.1 us
    all_to_all x1, waiting for transfers between devices, per_device(): lax.all_to_all(best.reshape(shards, capacity), 'shard', split_axis=0, con...  9.32 us
    all_to_all x1, waiting for transfers between devices, per_device(): lax.all_to_all(send_keys, 'shard', split_axis=0, concat_axis=0, tiled=True)  7.76 us
    all_to_all x1, starting transfers between devices, per_device(): lax.all_to_all(send_ids, 'shard', split_axis=0, concat_axis=0, tiled=True)  7.63 us
  transfers between devices with their start and end apart: 4, of which 4 were waited for; matrix products, arithmetic and copies ran while one was open for 3% of the time, Pallas kernels for 0%

commit v1 on v0

v1 whole, which is shorter than its diff:
```python
import functools
import math

import jax
import jax.numpy as jnp
from jax import lax
from jax.experimental import pallas as pl
from jax.experimental.pallas import tpu as pltpu
from jax.sharding import PartitionSpec as P

MESH = pl.DeviceIdType.MESH
PLANES = 8
PEERS = 32
GROUPS = 4
EMPTY = 2.0
FAR = -8.0

PAIRS = ((0, 1), (7, 2), (6, 3), (5, 4))
ORDER = (1, 7, 0, 2, 6, 3, 5, 4)


def iota(shape, dim):
    return lax.broadcasted_iota(jnp.int32, shape, dim)


def as_f32(mask):
    return mask.astype(jnp.float32)


def kernel(
    cap,
    emb_ref,
    clus_ref,
    valid_ref,
    out_ref,
    flag_ref,
    zsend,
    zmeta_send,
    zbuf,
    zmeta,
    psend,
    pbuf,
    bias,
    best,
    ret_send,
    ret_buf,
    zret_send,
    zret_buf,
    zs_sem,
    zr_sem,
    zms_sem,
    zmr_sem,
    ps_sem,
    pr_sem,
    loc_sem,
    rs_sem,
    rr_sem,
    zrs_sem,
    zrr_sem,
):
    docs, width = emb_ref.shape
    shard, blk = lax.axis_index("shard"), lax.axis_index("blk")
    my_z = shard // PLANES
    my_p = lax.rem(shard, PLANES) * 4 + blk

    def at(z, p):
        return (z * PLANES + p // 4, lax.rem(p, 4))

    def z_peer(d):
        return at(lax.rem(my_z + d, PLANES), my_p)

    def p_peer(p):
        return at(my_z, p)

    barrier = pltpu.get_barrier_semaphore()
    for d in range(1, PLANES):
        pl.semaphore_signal(barrier, inc=1, device_id=z_peer(d), device_id_type=MESH)

    def greet(i, carry):
        peer = lax.rem(my_p + i, PEERS)
        pl.semaphore_signal(barrier, inc=1, device_id=p_peer(peer), device_id_type=MESH)
        return carry

    lax.fori_loop(1, PEERS, greet, 0)

    clus = clus_ref[...]
    valid = valid_ref[...] > 0
    owner, sub = clus & 63, clus >> 6
    plane = ((owner >> 3) + 2 * sub) & (PLANES - 1)
    peer_of = (owner & 7) * 4 + sub
    rel = (plane - my_z + PLANES) & (PLANES - 1)
    rel_row = as_f32(jnp.where(valid, rel, -1))
    key_row = as_f32(jnp.where(valid, clus, -1))
    sub_i, lane_i = iota((docs, docs), 0), iota((docs, docs), 1)
    eye = sub_i == lane_i
    earlier = sub_i < lane_i

    def column(row):
        wide = jnp.broadcast_to(row, (docs, docs))
        return jnp.sum(jnp.where(eye, wide, 0.0), axis=1, keepdims=True)

    key_col, rel_col = column(key_row), column(rel_row)
    rank = jnp.sum(as_f32((key_col == key_row) & earlier), axis=0, keepdims=True)
    rank_z = jnp.sum(as_f32((rel_col == rel_row) & earlier), axis=0, keepdims=True)
    slot = as_f32(peer_of * 8) + rank
    slot_bf = jnp.broadcast_to(
        jnp.where(valid, slot + 1.0, 0.0), (8, docs)
    ).astype(jnp.bfloat16)
    fits = valid & (rank_z < float(cap))
    overflow = jnp.max(as_f32(valid & (rank_z >= float(cap))), axis=1, keepdims=True)
    target = jnp.where(fits, rel_row * float(cap) + rank_z, -1.0)

    values = emb_ref[...].astype(jnp.float32)
    scale = lax.rsqrt(jnp.mean(values * values, axis=1, keepdims=True) + 1e-05) / math.sqrt(width)
    unit = (values * scale).astype(jnp.bfloat16)

    pl.semaphore_wait(barrier, PLANES - 1 + PEERS - 1)

    def z_copies(d):
        g, h = place(d)
        rows = pltpu.make_async_remote_copy(
            src_ref=zsend.at[d],
            dst_ref=zbuf.at[g, h],
            send_sem=zs_sem.at[d],
            recv_sem=zr_sem.at[d],
            device_id=z_peer(d),
            device_id_type=MESH,
        )
        meta = pltpu.make_async_remote_copy(
            src_ref=zmeta_send.at[d],
            dst_ref=zmeta.at[d],
            send_sem=zms_sem.at[d],
            recv_sem=zmr_sem.at[d],
            device_id=z_peer(d),
            device_id_type=MESH,
        )
        return rows, meta

    lane128 = iota((1, 128), 1)
    for d in ORDER:
        g, h = place(d)
        pick = iota((cap, docs), 0).astype(jnp.float32) + float(d * cap) == target
        pick = as_f32(pick).astype(jnp.bfloat16)
        rows = jnp.dot(pick, unit, preferred_element_type=jnp.float32).astype(jnp.bfloat16)
        meta = lax.dot_general(
            slot_bf, pick, (((1,), (1,)), ((), ())), preferred_element_type=jnp.float32
        )[0:1, :]
        if d == 0:
            zbuf[g, h] = rows
            zmeta[d, :, 0:cap] = meta
            zmeta[d, :, 128:256] = jnp.broadcast_to(overflow, (1, 128))
        else:
            zsend[d] = rows
            zmeta_send[d, :, 0:cap] = meta
            zmeta_send[d, :, 128:256] = jnp.broadcast_to(overflow, (1, 128))
            row_copy, meta_copy = z_copies(d)
            meta_copy.start()
            row_copy.start()

    best[...] = jnp.full(best.shape, -1.0, jnp.float32)
    slot_lane = iota((PEERS * 8, cap), 0).astype(jnp.float32)
    flag = jnp.zeros((1, 128), jnp.float32)

    def scatter(g):
        picks = []
        flags = []
        for h, d in enumerate(PAIRS[g]):
            if d:
                row_copy, meta_copy = z_copies(d)
                meta_copy.wait_recv()
                row_copy.wait_recv()
            meta = zmeta[d, :, 0:cap]
            where_to = jnp.where(meta > 0.0, meta - 1.0 + float(4 * h), -1.0)
            picks.append(as_f32(slot_lane == where_to))
            flags.append(zmeta[d, :, 128:256])
        pick = jnp.concatenate(picks, axis=1)
        filled = jnp.sum(pick, axis=1, keepdims=True)
        rows = jnp.dot(
            pick.astype(jnp.bfloat16),
            zbuf[g].reshape(2 * cap, width),
            preferred_element_type=jnp.float32,
        )
        mark = jnp.where(iota((PEERS * 8, 128), 1) == 0, EMPTY * (1.0 - filled), 0.0)
        psend[g, :, :, 0:128] = (rows[:, 0:128] + mark).astype(jnp.bfloat16).reshape(PEERS, 8, 128)
        psend[g, :, :, 128:] = rows[:, 128:].astype(jnp.bfloat16).reshape(PEERS, 8, width - 128)
        local = pltpu.make_async_copy(psend.at[g, my_p], pbuf.at[g, my_p], loc_sem.at[g])
        local.start()

        def send(i, carry):
            peer = lax.rem(my_p + i, PEERS)
            pltpu.make_async_remote_copy(
                src_ref=psend.at[g, peer],
                dst_ref=pbuf.at[g, my_p],
                send_sem=ps_sem.at[g],
                recv_sem=pr_sem.at[g],
                device_id=p_peer(peer),
                device_id_type=MESH,
            ).start()
            return carry

        lax.fori_loop(1, PEERS, send, 0)
        return jnp.maximum(flags[0], flags[1])

    def all_in_plane(src, dst, send_sem, recv_sem):
        return pltpu.make_async_remote_copy(
            src_ref=src,
            dst_ref=dst,
            send_sem=send_sem,
            recv_sem=recv_sem,
            device_id=p_peer(lax.rem(my_p + 1, PEERS)),
            device_id_type=MESH,
        )

    def compare(g):
        pltpu.make_async_copy(psend.at[g, my_p], pbuf.at[g, my_p], loc_sem.at[g]).wait()
        all_in_plane(
            psend.at[g, pl.ds(0, PEERS - 1)],
            pbuf.at[g, pl.ds(0, PEERS - 1)],
            ps_sem.at[g],
            pr_sem.at[g],
        ).wait_recv()
        mine = pbuf[g].reshape(PEERS * 8, width)
        first = mine[:, 0:128].astype(jnp.float32)[:, 0:1]
        bias[g] = jnp.broadcast_to(jnp.where(first > 1.5, FAR, 0.0), (PEERS * 8, 128))

        def block(rows_j, rows_i, bias_j, i, same):
            similar = lax.dot_general(
                rows_j, rows_i, (((1,), (1,)), ((), ())), preferred_element_type=jnp.float32
            )
            similar = similar + jnp.concatenate([bias_j, bias_j], axis=1)
            if same:
                similar = jnp.where(eye, FAR, similar)
            best[i] = jnp.maximum(best[i], jnp.max(similar, axis=0, keepdims=True))

        block(mine, mine, bias[g], g, True)
        for j in range(g):
            other = pbuf[j].reshape(PEERS * 8, width)
            block(other, mine, bias[j], g, False)
            block(mine, other, bias[g], j, False)

    for g in range(GROUPS):
        flag = jnp.maximum(flag, scatter(g))
        if g:
            compare(g - 1)
    compare(GROUPS - 1)

    ret_send[...] = jnp.zeros(ret_send.shape, jnp.float32)
    for half in range(2):
        for g in range(GROUPS):
            ret_send[half, g : g + 1, :] = best[g, :, half * 128 : half * 128 + 128]
        ret_send[half, 4:5, :] = flag
    local = pltpu.make_async_copy(ret_send.at[my_p // 16], ret_buf.at[my_p], loc_sem.at[GROUPS])
    local.start()

    def send_back(i, carry):
        peer = lax.rem(my_p + i, PEERS)
        pltpu.make_async_remote_copy(
            src_ref=ret_send.at[peer // 16],
            dst_ref=ret_buf.at[my_p],
            send_sem=rs_sem,
            recv_sem=rr_sem,
            device_id=p_peer(peer),
            device_id_type=MESH,
        ).start()
        return carry

    lax.fori_loop(1, PEERS, send_back, 0)
    local.wait()
    all_in_plane(
        ret_buf.at[pl.ds(0, PEERS - 1)], ret_buf.at[pl.ds(0, PEERS - 1)], rs_sem, rr_sem
    ).wait()
    came = ret_buf[...]
    flag_ref[...] = jnp.max(came[:, 4, :], axis=0, keepdims=True)
    mine = iota((8, 128), 1) == 8 * lax.rem(my_p, 16) + iota((8, 128), 0)
    back = lax.dot_general(
        as_f32(mine),
        came.reshape(PEERS * 8, 128),
        (((1,), (1,)), ((), ())),
        precision=lax.Precision.HIGHEST,
        preferred_element_type=jnp.float32,
    )
    zret_buf[0] = back
    zret_send[...] = back

    def z_back(d):
        return pltpu.make_async_remote_copy(
            src_ref=zret_send,
            dst_ref=zret_buf.at[d],
            send_sem=zrs_sem.at[d],
            recv_sem=zrr_sem.at[d],
            device_id=z_peer(PLANES - d),
            device_id_type=MESH,
        )

    for d in range(1, PLANES):
        z_back(d).start()

    upper = (rel >= 1) & (rel <= 4)
    group = jnp.where(upper, rel - 1, (PLANES - rel) & 7)
    lane_of = as_f32(peer_of * 8 + group)
    row_of = as_f32(rel * 8 + jnp.where(upper, 4, 0)) + rank
    look = as_f32(sub_i.astype(jnp.float32) == lane_of)
    for d in range(1, PLANES):
        z_back(d).wait_recv()
    found = jnp.dot(
        zret_buf[...].reshape(PLANES * 8, PEERS * 8),
        look,
        precision=lax.Precision.HIGHEST,
        preferred_element_type=jnp.float32,
    )
    right = iota((PLANES * 8, docs), 0).astype(jnp.float32) == row_of
    found = jnp.sum(jnp.where(right, found, 0.0), axis=0, keepdims=True)
    out_ref[...] = jnp.where(valid, jnp.maximum(found, -1.0), -1.0)

    for d in range(1, PLANES):
        row_copy, meta_copy = z_copies(d)
        row_copy.wait_send()
        meta_copy.wait_send()
        z_back(d).wait_send()
    for g in range(GROUPS):
        all_in_plane(
            psend.at[g, pl.ds(0, PEERS - 1)],
            pbuf.at[g, pl.ds(0, PEERS - 1)],
            ps_sem.at[g],
            pr_sem.at[g],
        ).wait_send()


def place(d):
    for g, pair in enumerate(PAIRS):
        if d in pair:
            return g, pair.index(d)


def route(cap, collective_id, embeddings, cluster, valid):
    docs, width = embeddings.shape
    vmem = pl.BlockSpec(memory_space=pltpu.VMEM)
    dma = pltpu.SemaphoreType.DMA
    return pl.pallas_call(
        functools.partial(kernel, cap),
        out_shape=(
            jax.ShapeDtypeStruct((1, docs), jnp.float32),
            jax.ShapeDtypeStruct((1, 128), jnp.float32),
        ),
        in_specs=[vmem] * 3,
        out_specs=(vmem, vmem),
        scratch_shapes=[
            pltpu.VMEM((PLANES, cap, width), jnp.bfloat16),
            pltpu.VMEM((PLANES, 1, 256), jnp.float32),
            pltpu.VMEM((GROUPS, 2, cap, width), jnp.bfloat16),
            pltpu.VMEM((PLANES, 1, 256), jnp.float32),
            pltpu.VMEM((GROUPS, PEERS, 8, width), jnp.bfloat16),
            pltpu.VMEM((GROUPS, PEERS, 8, width), jnp.bfloat16),
            pltpu.VMEM((GROUPS, PEERS * 8, 128), jnp.float32),
            pltpu.VMEM((GROUPS, 1, PEERS * 8), jnp.float32),
            pltpu.VMEM((2, 8, 128), jnp.float32),
            pltpu.VMEM((PEERS, 8, 128), jnp.float32),
            pltpu.VMEM((8, PEERS * 8), jnp.float32),
            pltpu.VMEM((PLANES, 8, PEERS * 8), jnp.float32),
            dma((PLANES,)),
            dma((PLANES,)),
            dma((PLANES,)),
            dma((PLANES,)),
            dma((GROUPS,)),
            dma((GROUPS,)),
            dma((GROUPS + 1,)),
            dma(()),
            dma(()),
            dma((PLANES,)),
            dma((PLANES,)),
        ],
        compiler_params=pltpu.CompilerParams(
            collective_id=collective_id, has_side_effects=True, vmem_limit_bytes=40 << 20
        ),
        name=f"route_{cap}",
    )(embeddings, cluster, valid)


def per_device(embeddings, doc_cluster, doc_valid):
    docs = embeddings.shape[0]
    best, _ = route(128, 0, embeddings, doc_cluster.reshape(1, docs), doc_valid.reshape(1, docs))
    return best.reshape(docs)


def solution(mesh):
    placed = (P(("shard", "blk"), None), P(("shard", "blk")), P(("shard", "blk")))
    return jax.shard_map(
        per_device, mesh=mesh, in_specs=placed, out_specs=P(("shard", "blk")), check_vma=False
    )
```

time: 188 us -> 82.9 us (0.44)
  Pallas kernels: 0 us -> 80.5 us
  blocking collectives: 79.7 us -> 0 us
  waiting for transfers between devices: 38.4 us -> 0 us
  starting transfers between devices: 22.3 us -> 0 us
  matrix products: 16.1 us -> 0 us
  between operations: 13.5 us -> 0.01 us
  other arithmetic: 7.88 us -> 0 us
  local copies, waits for them, and re-layouts: 9.96 us -> 2.3 us
    pallas_call x0 -> x1, Pallas kernels: none -> 80.5 us  [route(): pl.pallas_call(functools.partial(kernel, cap), out_shape=(jax.ShapeDtypeS...]
    all_to_all x1 -> x0, blocking collectives: 61.9 us -> none  [per_device(): lax.all_to_all(send_rows, 'shard', split_axis=0, concat_axis=0, tiled=True)]
    all_to_all x3 -> x0, waiting for transfers between devices: 24.3 us -> none  [the longest x1 9.32 us: per_device(): lax.all_to_all(best.reshape(shards, capacity), 'shard', split_axis=0, con...]
    all_to_all x3 -> x0, starting transfers between devices: 22.3 us -> none  [the longest x1 10.1 us: per_device(): lax.all_to_all(best.reshape(shards, capacity), 'shard', split_axis=0, con...]
    all_gather x2 -> x0, blocking collectives: 17.8 us -> none  [the longest x1 10.9 us: per_device(): lax.all_gather(query_ids, 'blk', axis=0, tiled=True)]
    dot_general x8 -> x0, matrix products: 16.1 us -> none  [one_block(): lax.dot_general(rows_part, rows_key, (((1,), (1,)), ((), ())), preferred_...]
    all_gather x1 -> x0, waiting for transfers between devices: 14.1 us -> none  [per_device(): lax.all_gather(query_rows, 'blk', axis=0, tiled=True)]
    scatter x1 -> x0, other arithmetic: 2.9 us -> none  [per_device(): jnp.zeros((slots, width), jnp.bfloat16).at[slot_of]]
  transfers between devices with their start and end apart: 4 -> 0, of which waited for: 4 -> 0; matrix products, arithmetic and copies ran while one was open for 3% -> 0% of each run, Pallas kernels for 0% -> 0%
where the time goes in v1:
time: 82.9 us; the launch traced here: 82.8 us
  Pallas kernels  80.5 us (97%)
  local copies, waits for them, and re-layouts  2.3 us (3%)
    pallas_call x1, Pallas kernels, route(): pl.pallas_call(functools.partial(kernel, cap), out_shape=(jax.ShapeDtypeS...  80.5 us
    unnamed x7, local copies, waits for them, and re-layouts  2.3 us

profile of v1, /device:TPU:1, one launch (start us, length us, event | category | flops | bytes accessed | tf_op | source)
XLA Modules:
  0.0 82.8 jit_solution(14942978448026128344)
XLA Ops:
  0.0 0.0 copy-start.2
  0.0 0.0 copy-start.1
  0.0 0.7 copy-done.2
  0.7 0.0 copy-done.1
  0.7 0.0 copy-start
  0.7 1.0 %copy-done = bf16[256,1024]{1,0:T(8,128)(2,1)S(1)} copy-done((bf16[256,1024]{1,0:T(8,128)(2,1)S(1)}, bf16[256,1024]{1,0:T(8,128)(2,1)}, u32[]{:S(2)}) %copy-start) | copy-done | bytes 524312
  1.7 80.5 %route_128.1 = (f32[1,256]{1,0:T(1,128)S(1)}, f32[1,128]{1,0:T(1,128)}) custom-call(bf16[256,1024]{1,0:T(8,128)(2,1)S(1)} %copy-done, s32[1,256]{1,0:T(1,128)S(1)} %bitcast.3, s32[1,256]{1,0:T(1,128)S(1)} %bitcast.4), custom_call_target="tpu_custom_call" | custom-call | tf_op jit(solution)/shard_map/route_128/pallas_call | solution.py:339
  82.2 0.6 copy.5
Async XLA Ops:
  0.0 0.7 copy-start.2
  0.0 0.7 copy-start.1
  0.7 1.0 %copy-start = (bf16[256,1024]{1,0:T(8,128)(2,1)S(1)}, bf16[256,1024]{1,0:T(8,128)(2,1)}, u32[]{:S(2)}) copy-start(bf16[256,1024]{1,0:T(8,128)(2,1)} %emb_ref.1) | copy-start | bytes 1572868

commit v2 on v1

--- a/solution.py
+++ b/solution.py
@@ -15,6 +15,9 @@
 EMPTY = 2.0
 FAR = -8.0
 
+CAP = 56
+MOST = 128
+
 PAIRS = ((0, 1), (7, 2), (6, 3), (5, 4))
 ORDER = (1, 7, 0, 2, 6, 3, 5, 4)
 
@@ -29,11 +32,14 @@
 
 def kernel(
     cap,
+    emb_hbm,
+    clus_hbm,
+    valid_hbm,
+    out_ref,
+    flag_ref,
     emb_ref,
     clus_ref,
     valid_ref,
-    out_ref,
-    flag_ref,
     zsend,
     zmeta_send,
     zbuf,
@@ -57,6 +63,7 @@
     rr_sem,
     zrs_sem,
     zrr_sem,
+    in_sem,
 ):
     docs, width = emb_ref.shape
     shard, blk = lax.axis_index("shard"), lax.axis_index("blk")
@@ -72,6 +79,15 @@
     def p_peer(p):
         return at(my_z, p)
 
+    loads = [
+        pltpu.make_async_copy(src, dst, in_sem.at[i])
+        for i, (src, dst) in enumerate(
+            ((emb_hbm, emb_ref), (clus_hbm, clus_ref), (valid_hbm, valid_ref))
+        )
+    ]
+    for load in loads:
+        load.start()
+
     barrier = pltpu.get_barrier_semaphore()
     for d in range(1, PLANES):
         pl.semaphore_signal(barrier, inc=1, device_id=z_peer(d), device_id_type=MESH)
@@ -83,6 +99,8 @@
 
     lax.fori_loop(1, PEERS, greet, 0)
 
+    for load in loads:
+        load.wait()
     clus = clus_ref[...]
     valid = valid_ref[...] > 0
     owner, sub = clus & 63, clus >> 6
@@ -240,9 +258,8 @@
 
     for g in range(GROUPS):
         flag = jnp.maximum(flag, scatter(g))
-        if g:
-            compare(g - 1)
-    compare(GROUPS - 1)
+    for g in range(GROUPS):
+        compare(g)
 
     ret_send[...] = jnp.zeros(ret_send.shape, jnp.float32)
     for half in range(2):
@@ -342,9 +359,12 @@
             jax.ShapeDtypeStruct((1, docs), jnp.float32),
             jax.ShapeDtypeStruct((1, 128), jnp.float32),
         ),
-        in_specs=[vmem] * 3,
+        in_specs=[pl.BlockSpec(memory_space=pl.ANY)] * 3,
         out_specs=(vmem, vmem),
         scratch_shapes=[
+            pltpu.VMEM((docs, width), jnp.bfloat16),
+            pltpu.VMEM((1, docs), jnp.int32),
+            pltpu.VMEM((1, docs), jnp.int32),
             pltpu.VMEM((PLANES, cap, width), jnp.bfloat16),
             pltpu.VMEM((PLANES, 1, 256), jnp.float32),
             pltpu.VMEM((GROUPS, 2, cap, width), jnp.bfloat16),
@@ -368,6 +388,7 @@
             dma(()),
             dma((PLANES,)),
             dma((PLANES,)),
+            dma((3,)),
         ],
         compiler_params=pltpu.CompilerParams(
             collective_id=collective_id, has_side_effects=True, vmem_limit_bytes=40 << 20
@@ -378,7 +399,9 @@
 
 def per_device(embeddings, doc_cluster, doc_valid):
     docs = embeddings.shape[0]
-    best, _ = route(128, 0, embeddings, doc_cluster.reshape(1, docs), doc_valid.reshape(1, docs))
+    args = (embeddings, doc_cluster.reshape(1, docs), doc_valid.reshape(1, docs))
+    best, flag = route(CAP, 0, *args)
+    best = lax.cond(flag[0, 0] > 0.0, lambda: route(MOST, 1, *args)[0], lambda: best)
     return best.reshape(docs)
 
 

time: 82.9 us -> 57.4 us (0.69)
  Pallas kernels: 80.5 us -> 56 us
  local copies, waits for them, and re-layouts: 2.3 us -> 1.23 us
    pallas_call x1, Pallas kernels: 80.5 us -> 56 us  [route(): pl.pallas_call(functools.partial(kernel, cap), out_shape=(jax.ShapeDtypeS...]
    unnamed x7, local copies, waits for them, and re-layouts: 2.3 us -> 1.23 us
where the time goes in v2:
time: 57.4 us; the launch traced here: 57.3 us
  Pallas kernels  56 us (98%)
  local copies, waits for them, and re-layouts  1.23 us (2%)
    pallas_call x1, Pallas kernels, route(): pl.pallas_call(functools.partial(kernel, cap), out_shape=(jax.ShapeDtypeS...  56 us
    unnamed x7, local copies, waits for them, and re-layouts  1.23 us

profile of v2, /device:TPU:1, one launch (start us, length us, event | category | flops | bytes accessed | tf_op | source)
XLA Modules:
  0.0 57.3 jit_solution(6707695058528273719)
XLA Ops:
  0.0 0.0 copy-start
  0.0 56.0 %route_56.1 = (f32[1,256]{1,0:T(1,128)S(1)}, f32[1,128]{1,0:T(1,128)S(1)}) custom-call(bf16[256,1024]{1,0:T(8,128)(2,1)} %emb_hbm.1, s32[1,256]{1,0:T(1,128)} %bitcast.7, s32[1,256]{1,0:T(1,128)} %bitcast.9), custom_call_target="tpu_custom_call" | custom-call | tf_op jit(solution)/shard_map/route_56/pallas_call | solution.py:356
  56.0 0.0 copy-start.2
  56.0 0.0 copy-start.1
  56.0 0.0 copy-done
  56.0 0.6 %copy-done.2 = s32[256]{0:T(256)S(1)} copy-done((s32[256]{0:T(256)S(1)}, s32[256]{0:T(256)}, u32[]{:S(2)}) %copy-start.2) | copy-done | bytes 1048
  56.6 0.0 copy-done.1
  56.7 0.6 copy.10
  (1 shorter events, 0.0 us)
Async XLA Ops:
  0.0 56.0 %copy-start = (bf16[256,1024]{1,0:T(8,128)(2,1)S(1)}, bf16[256,1024]{1,0:T(8,128)(2,1)}, u32[]{:S(2)}) copy-start(bf16[256,1024]{1,0:T(8,128)(2,1)} %emb_hbm.1) | copy-start | bytes 1572868
  56.0 0.7 %copy-start.2 = (s32[256]{0:T(256)S(1)}, s32[256]{0:T(256)}, u32[]{:S(2)}) copy-start(s32[256]{0:T(256)} %param.7) | copy-start | bytes 3076
  56.0 0.7 %copy-start.1 = (s32[256]{0:T(256)S(1)}, s32[256]{0:T(256)}, u32[]{:S(2)}) copy-start(s32[256]{0:T(256)} %param.6) | copy-start | bytes 3076

commit v3 on v2

v3 whole, which is shorter than its diff:
```python
import functools
import math

import jax
import jax.numpy as jnp
from jax import lax
from jax.experimental import pallas as pl
from jax.experimental.pallas import tpu as pltpu
from jax.sharding import PartitionSpec as P

MESH = pl.DeviceIdType.MESH
PLANES = 8
PEERS = 32
EMPTY = 2.0
FAR = -8.0

CAP = 56
MOST = 128

GROUPS = ((0,), (1, 7), (2, 6), (3, 5), (4,))
ORDER = (1, 7, 0, 2, 6, 3, 5, 4)
PLACE = {d: i for i, d in enumerate(d for group in GROUPS for d in group)}


def iota(shape, dim):
    return lax.broadcasted_iota(jnp.int32, shape, dim)


def as_f32(mask):
    return mask.astype(jnp.float32)


def parts(values):
    high = values.astype(jnp.bfloat16)
    rest = values - high.astype(jnp.float32)
    middle = rest.astype(jnp.bfloat16)
    low = (rest - middle.astype(jnp.float32)).astype(jnp.bfloat16)
    return jnp.concatenate([high, middle, low], axis=0)


def kernel(
    cap,
    emb_hbm,
    clus_hbm,
    valid_hbm,
    out_ref,
    flag_ref,
    clus_out,
    valid_out,
    emb_ref,
    clus_ref,
    valid_ref,
    zsend,
    zmeta_send,
    zbuf,
    zmeta,
    psends,
    pbufs,
    biases,
    bests,
    ret_send,
    ret_buf,
    zret_send,
    zret_buf,
    zs_sem,
    zr_sem,
    zms_sem,
    zmr_sem,
    ps_sem,
    pr_sem,
    loc_sem,
    rs_sem,
    rr_sem,
    zrs_sem,
    zrr_sem,
    in_sem,
):
    docs, width = emb_ref.shape
    shard, blk = lax.axis_index("shard"), lax.axis_index("blk")
    my_z = shard // PLANES
    my_p = lax.rem(shard, PLANES) * 4 + blk

    def at(z, p):
        return (z * PLANES + p // 4, lax.rem(p, 4))

    def z_peer(d):
        return at(lax.rem(my_z + d, PLANES), my_p)

    def p_peer(p):
        return at(my_z, p)

    loads = [
        pltpu.make_async_copy(src, dst, in_sem.at[i])
        for i, (src, dst) in enumerate(
            ((emb_hbm, emb_ref), (clus_hbm, clus_ref), (valid_hbm, valid_ref))
        )
    ]
    for load in loads:
        load.start()

    barrier = pltpu.get_barrier_semaphore()
    for d in range(1, PLANES):
        pl.semaphore_signal(barrier, inc=1, device_id=z_peer(d), device_id_type=MESH)

    def greet(i, carry):
        peer = lax.rem(my_p + i, PEERS)
        pl.semaphore_signal(barrier, inc=1, device_id=p_peer(peer), device_id_type=MESH)
        return carry

    lax.fori_loop(1, PEERS, greet, 0)

    for load in loads[1:]:
        load.wait()
    clus = clus_ref[...]
    valid = valid_ref[...] > 0
    clus_out[...] = clus
    valid_out[...] = valid_ref[...]
    owner, sub = clus & 63, clus >> 6
    plane = ((owner >> 3) + 2 * sub) & (PLANES - 1)
    peer_of = (owner & 7) * 4 + sub
    rel = (plane - my_z + PLANES) & (PLANES - 1)
    rel_row = as_f32(jnp.where(valid, rel, -1))
    key_row = as_f32(jnp.where(valid, clus, -1))
    sub_i, lane_i = iota((docs, docs), 0), iota((docs, docs), 1)
    eye = sub_i == lane_i
    earlier = sub_i < lane_i

    def column(row):
        wide = jnp.broadcast_to(row, (docs, docs))
        return jnp.sum(jnp.where(eye, wide, 0.0), axis=1, keepdims=True)

    key_col, rel_col = column(key_row), column(rel_row)
    rank = jnp.sum(as_f32((key_col == key_row) & earlier), axis=0, keepdims=True)
    rank_z = jnp.sum(as_f32((rel_col == rel_row) & earlier), axis=0, keepdims=True)
    slot = {
        n: jnp.broadcast_to(
            jnp.where(valid, as_f32(peer_of * n) + rank + 1.0, 0.0), (8, docs)
        ).astype(jnp.bfloat16)
        for n in (4, 8)
    }
    fits = valid & (rank_z < float(cap))
    overflow = jnp.max(as_f32(valid & (rank_z >= float(cap))), axis=1, keepdims=True)
    target = jnp.where(fits, rel_row * float(cap) + rank_z, -1.0)

    loads[0].wait()
    values = emb_ref[...].astype(jnp.float32)
    scale = lax.rsqrt(jnp.mean(values * values, axis=1, keepdims=True) + 1e-05) / math.sqrt(width)
    unit = (values * scale).astype(jnp.bfloat16)

    pl.semaphore_wait(barrier, PLANES - 1 + PEERS - 1)

    def z_copies(d):
        rows = pltpu.make_async_remote_copy(
            src_ref=zsend.at[d],
            dst_ref=zbuf.at[PLACE[d]],
            send_sem=zs_sem.at[d],
            recv_sem=zr_sem.at[d],
            device_id=z_peer(d),
            device_id_type=MESH,
        )
        meta = pltpu.make_async_remote_copy(
            src_ref=zmeta_send.at[d],
            dst_ref=zmeta.at[d],
            send_sem=zms_sem.at[d],
            recv_sem=zmr_sem.at[d],
            device_id=z_peer(d),
            device_id_type=MESH,
        )
        return rows, meta

    lane128 = iota((1, 128), 1)
    for d in ORDER:
        pick = iota((cap, docs), 0).astype(jnp.float32) + float(d * cap) == target
        pick = as_f32(pick).astype(jnp.bfloat16)
        rows = jnp.dot(pick, unit, preferred_element_type=jnp.float32).astype(jnp.bfloat16)
        meta = lax.dot_general(
            slot[4 if d in (0, 4) else 8], pick, (((1,), (1,)), ((), ())), preferred_element_type=jnp.float32
        )[0:1, :]
        if d == 0:
            zbuf[PLACE[d]] = rows
            zmeta[d, :, 0:cap] = meta
            zmeta[d, :, 128:256] = jnp.broadcast_to(overflow, (1, 128))
        else:
            zsend[d] = rows
            zmeta_send[d, :, 0:cap] = meta
            zmeta_send[d, :, 128:256] = jnp.broadcast_to(overflow, (1, 128))
            row_copy, meta_copy = z_copies(d)
            if d != 4:
                meta_copy.start()
                row_copy.start()

    for best in bests:
        best[...] = jnp.full(best.shape, -1.0, jnp.float32)
    flag = jnp.zeros((1, 128), jnp.float32)

    def scatter(g):
        picks = []
        flags = []
        psend, pbuf = psends[g], pbufs[g]
        slots = psend.shape[1]
        slot_lane = iota((PEERS * slots, cap), 0).astype(jnp.float32)
        for h, d in enumerate(GROUPS[g]):
            if d:
                row_copy, meta_copy = z_copies(d)
                meta_copy.wait_recv()
                row_copy.wait_recv()
            meta = zmeta[d, :, 0:cap]
            where_to = jnp.where(meta > 0.0, meta - 1.0 + float(4 * h), -1.0)
            picks.append(as_f32(slot_lane == where_to))
            flags.append(zmeta[d, :, 128:256])
        pick = jnp.concatenate(picks, axis=1) if len(picks) > 1 else picks[0]
        filled = jnp.sum(pick, axis=1, keepdims=True)
        rows = jnp.dot(
            pick.astype(jnp.bfloat16),
            zbuf[PLACE[GROUPS[g][0]] : PLACE[GROUPS[g][-1]] + 1].reshape(len(picks) * cap, width),
            preferred_element_type=jnp.float32,
        )
        mark = jnp.where(iota((PEERS * slots, 128), 1) == 0, EMPTY * (1.0 - filled), 0.0)
        head = (rows[:, 0:128] + mark).astype(jnp.bfloat16)
        psend[:, :, 0:128] = head.reshape(PEERS, slots, 128)
        tail = rows[:, 128:].astype(jnp.bfloat16)
        psend[:, :, 128:] = tail.reshape(PEERS, slots, width - 128)
        local = pltpu.make_async_copy(psend.at[my_p], pbuf.at[my_p], loc_sem.at[g])
        local.start()

        def send(i, carry):
            peer = lax.rem(my_p + i, PEERS)
            pltpu.make_async_remote_copy(
                src_ref=psend.at[peer],
                dst_ref=pbuf.at[my_p],
                send_sem=ps_sem.at[g],
                recv_sem=pr_sem.at[g],
                device_id=p_peer(peer),
                device_id_type=MESH,
            ).start()
            return carry

        lax.fori_loop(1, PEERS, send, 0)
        return functools.reduce(jnp.maximum, flags)

    def all_in_plane(src, dst, send_sem, recv_sem):
        return pltpu.make_async_remote_copy(
            src_ref=src,
            dst_ref=dst,
            send_sem=send_sem,
            recv_sem=recv_sem,
            device_id=p_peer(lax.rem(my_p + 1, PEERS)),
            device_id_type=MESH,
        )

    def in_plane(g):
        return all_in_plane(
            psends[g].at[pl.ds(0, PEERS - 1)],
            pbufs[g].at[pl.ds(0, PEERS - 1)],
            ps_sem.at[g],
            pr_sem.at[g],
        )

    def rows_of(g):
        return pbufs[g][...].reshape(-1, width)

    def compare(g):
        pltpu.make_async_copy(psends[g].at[my_p], pbufs[g].at[my_p], loc_sem.at[g]).wait()
        in_plane(g).wait_recv()
        mine = rows_of(g)
        first = mine[:, 0:128].astype(jnp.float32)[:, 0:1]
        biases[g][...] = jnp.broadcast_to(jnp.where(first > 1.5, FAR, 0.0), biases[g].shape)

        def block(rows_j, rows_i, j, i):
            similar = lax.dot_general(
                rows_j, rows_i, (((1,), (1,)), ((), ())), preferred_element_type=jnp.float32
            )
            away = biases[j][...]
            if rows_i.shape[0] > 128:
                away = jnp.concatenate([away, away], axis=1)
            similar = similar + away
            if i == j:
                same = iota(similar.shape, 0) == iota(similar.shape, 1)
                similar = jnp.where(same, FAR, similar)
            bests[i][...] = jnp.maximum(bests[i][...], jnp.max(similar, axis=0, keepdims=True))

        block(mine, mine, g, g)
        for j in range(g):
            other = rows_of(j)
            block(other, mine, j, g)
            block(mine, other, g, j)

    for g in range(len(GROUPS)):
        if g == len(GROUPS) - 1:
            compare(0)
            compare(1)
        if g == 2:
            for copy in z_copies(4):
                copy.start()
        flag = jnp.maximum(flag, scatter(g))
    for g in range(2, len(GROUPS)):
        compare(g)

    ret_send[...] = jnp.zeros(ret_send.shape, jnp.float32)
    for half in range(2):
        for g, best in enumerate(bests):
            first = half * 128 if best.shape[1] > 128 else 0
            ret_send[half, g : g + 1, :] = best[:, first : first + 128]
        ret_send[half, 5:6, :] = flag
    local = pltpu.make_async_copy(ret_send.at[my_p // 16], ret_buf.at[my_p], loc_sem.at[len(GROUPS)])
    local.start()

    def send_back(i, carry):
        peer = lax.rem(my_p + i, PEERS)
        pltpu.make_async_remote_copy(
            src_ref=ret_send.at[peer // 16],
            dst_ref=ret_buf.at[my_p],
            send_sem=rs_sem,
            recv_sem=rr_sem,
            device_id=p_peer(peer),
            device_id_type=MESH,
        ).start()
        return carry

    lax.fori_loop(1, PEERS, send_back, 0)
    number, lane = iota((16, 128), 0), iota((16, 128), 1)
    mine = jnp.where(
        number < 8,
        as_f32(lane == 8 * lax.rem(my_p, 16) + number),
        as_f32((lane == 4 * my_p + number - 8) & (number < 12)),
    ).astype(jnp.bfloat16)
    local.wait()
    all_in_plane(
        ret_buf.at[pl.ds(0, PEERS - 1)], ret_buf.at[pl.ds(0, PEERS - 1)], rs_sem, rr_sem
    ).wait_recv()
    came = ret_buf[...]
    flag_ref[...] = jnp.max(came[:, 5, :], axis=0, keepdims=True)
    back = lax.dot_general(
        mine,
        parts(came.reshape(PEERS * 8, 128)),
        (((1,), (1,)), ((), ())),
        preferred_element_type=jnp.float32,
    )
    back = back[:, 0:256] + back[:, 256:512] + back[:, 512:768]
    group = iota((8, PEERS * 8), 1) & 7
    alone = (group == 0) | (group == len(GROUPS) - 1)
    back = jnp.where(alone, back[8:16], back[0:8])
    zret_buf[0] = back
    zret_send[...] = back

    def z_back(d):
        return pltpu.make_async_remote_copy(
            src_ref=zret_send,
            dst_ref=zret_buf.at[d],
            send_sem=zrs_sem.at[d],
            recv_sem=zrr_sem.at[d],
            device_id=z_peer(PLANES - d),
            device_id_type=MESH,
        )

    for d in range(1, PLANES):
        z_back(d).start()

    upper = rel > 4
    lane_of = as_f32(peer_of * 8 + jnp.where(upper, PLANES - rel, rel))
    row_of = as_f32(rel * 8 + jnp.where(upper, 4, 0)) + rank
    look = as_f32(sub_i.astype(jnp.float32) == lane_of).astype(jnp.bfloat16)
    for d in range(1, PLANES):
        z_back(d).wait_recv()
    found = jnp.dot(
        parts(zret_buf[...].reshape(PLANES * 8, PEERS * 8)),
        look,
        preferred_element_type=jnp.float32,
    )
    found = found[0:64] + found[64:128] + found[128:192]
    right = iota((PLANES * 8, docs), 0).astype(jnp.float32) == row_of
    found = jnp.sum(jnp.where(right, found, 0.0), axis=0, keepdims=True)
    out_ref[...] = jnp.where(valid, jnp.maximum(found, -1.0), -1.0)

    for d in range(1, PLANES):
        row_copy, meta_copy = z_copies(d)
        row_copy.wait_send()
        meta_copy.wait_send()
        z_back(d).wait_send()
    for g in range(len(GROUPS)):
        in_plane(g).wait_send()
    all_in_plane(
        ret_buf.at[pl.ds(0, PEERS - 1)], ret_buf.at[pl.ds(0, PEERS - 1)], rs_sem, rr_sem
    ).wait_send()


def route(cap, collective_id, space, embeddings, cluster, valid):
    docs, width = embeddings.shape
    vmem = pl.BlockSpec(memory_space=pltpu.VMEM)
    dma = pltpu.SemaphoreType.DMA
    slots = [4 * len(group) for group in GROUPS]
    return pl.pallas_call(
        functools.partial(kernel, cap),
        out_shape=(
            jax.ShapeDtypeStruct((1, docs), jnp.float32),
            jax.ShapeDtypeStruct((1, 128), jnp.float32),
            jax.ShapeDtypeStruct((1, docs), jnp.int32),
            jax.ShapeDtypeStruct((1, docs), jnp.int32),
        ),
        in_specs=[pl.BlockSpec(memory_space=space)] * 3,
        out_specs=(vmem,) * 4,
        scratch_shapes=[
            pltpu.VMEM((docs, width), jnp.bfloat16),
            pltpu.VMEM((1, docs), jnp.int32),
            pltpu.VMEM((1, docs), jnp.int32),
            pltpu.VMEM((PLANES, cap, width), jnp.bfloat16),
            pltpu.VMEM((PLANES, 1, 256), jnp.float32),
            pltpu.VMEM((PLANES, cap, width), jnp.bfloat16),
            pltpu.VMEM((PLANES, 1, 256), jnp.float32),
            [pltpu.VMEM((PEERS, n, width), jnp.bfloat16) for n in slots],
            [pltpu.VMEM((PEERS, n, width), jnp.bfloat16) for n in slots],
            [pltpu.VMEM((PEERS * n, 128), jnp.float32) for n in slots],
            [pltpu.VMEM((1, PEERS * n), jnp.float32) for n in slots],
            pltpu.VMEM((2, 8, 128), jnp.float32),
            pltpu.VMEM((PEERS, 8, 128), jnp.float32),
            pltpu.VMEM((8, PEERS * 8), jnp.float32),
            pltpu.VMEM((PLANES, 8, PEERS * 8), jnp.float32),
            dma((PLANES,)),
            dma((PLANES,)),
            dma((PLANES,)),
            dma((PLANES,)),
            dma((len(GROUPS),)),
            dma((len(GROUPS),)),
            dma((len(GROUPS) + 1,)),
            dma(()),
            dma(()),
            dma((PLANES,)),
            dma((PLANES,)),
            dma((3,)),
        ],
        compiler_params=pltpu.CompilerParams(
            collective_id=collective_id, has_side_effects=True, vmem_limit_bytes=40 << 20
        ),
        name=f"route_{cap}",
    )(embeddings, cluster, valid)


def per_device(embeddings, doc_cluster, doc_valid):
    docs = embeddings.shape[0]
    cluster, valid = doc_cluster.reshape(1, docs), doc_valid.reshape(1, docs)
    hbm = [pltpu.with_memory_space_constraint(a, pltpu.HBM) for a in (embeddings, cluster, valid)]
    best, flag, cluster, valid = route(CAP, 0, pltpu.HBM, *hbm)
    best = lax.cond(
        flag[0, 0] > 0.0,
        lambda: route(MOST, 1, pl.ANY, embeddings, cluster, valid)[0],
        lambda: best,
    )
    return best.reshape(docs)


def solution(mesh):
    placed = (P(("shard", "blk"), None), P(("shard", "blk")), P(("shard", "blk")))
    return jax.shard_map(
        per_device, mesh=mesh, in_specs=placed, out_specs=P(("shard", "blk")), check_vma=False
    )
```

time: 57.4 us -> 55.1 us (0.960)
  Pallas kernels: 56 us -> 54.2 us
  local copies, waits for them, and re-layouts: 1.23 us -> 0.57 us
    pallas_call x1, Pallas kernels: 56 us -> 54.2 us  [route(): pl.pallas_call(functools.partial(kernel, cap), out_shape=(jax.ShapeDtypeS...]
    unnamed x7 -> x3, local copies, waits for them, and re-layouts: 1.23 us -> 0.57 us
where the time goes in v3:
time: 55.1 us; the launch traced here: 55 us
  Pallas kernels  54.2 us (98%)
  local copies, waits for them, and re-layouts  0.57 us (1%)
    pallas_call x1, Pallas kernels, route(): pl.pallas_call(functools.partial(kernel, cap), out_shape=(jax.ShapeDtypeS...  54.2 us

profile of v3, /device:TPU:1, one launch (start us, length us, event | category | flops | bytes accessed | tf_op | source)
XLA Modules:
  0.0 55.0 jit_solution(3277498948365912138)
XLA Ops:
  0.0 0.0 copy-start
  0.0 54.2 %route_56.1 = (f32[1,256]{1,0:T(1,128)S(1)}, f32[1,128]{1,0:T(1,128)S(1)}, s32[1,256]{1,0:T(1,128)S(1)}, s32[1,256]{1,0:T(1,128)S(1)}) custom-call(bf16[256,1024]{1,0:T(8,128)(2,1)} %emb_hbm.1, s32[1,256]{1,0:T(1,128)} %bitcast.7, s32[1,256]{1,0:T(1,128)} %bitcast.8), custom_call_target="tpu_custom_call" | custom-call | tf_op jit(solution)/shard_map/route_56/pallas_call | solution.py:392
  54.2 0.0 copy-done
  54.2 0.2 conditional.1
  54.4 0.6 %copy.10 = f32[256]{0:T(256)} copy(f32[256]{0:T(256)S(1)} %get-tuple-element.29) | data formatting | bytes 2048
Async XLA Ops:
  0.0 54.2 %copy-start = (bf16[256,1024]{1,0:T(8,128)(2,1)S(1)}, bf16[256,1024]{1,0:T(8,128)(2,1)}, u32[]{:S(2)}) copy-start(bf16[256,1024]{1,0:T(8,128)(2,1)} %emb_hbm.1) | copy-start | bytes 1572868

commit v4 on v3

--- a/solution.py
+++ b/solution.py
@@ -17,6 +17,10 @@
 CAP = 56
 MOST = 128
 
+STEPS = sorted(
+    ((x, y, core) for x in range(4) for y in range(4) for core in range(2) if (x, y, core) != (0, 0, 0)),
+    key=lambda step: (-min(step[0], 4 - step[0]) - min(step[1], 4 - step[1]), step),
+)
 GROUPS = ((0,), (1, 7), (2, 6), (3, 5), (4,))
 ORDER = (1, 7, 0, 2, 6, 3, 5, 4)
 PLACE = {d: i for i, d in enumerate(d for group in GROUPS for d in group)}
@@ -98,6 +102,14 @@
     for load in loads:
         load.start()
 
+    my_x = lax.rem(my_p // 2, 2) * 2 + my_p // 16
+    my_y, my_core = lax.rem(my_p // 4, 4), lax.rem(my_p, 2)
+
+    def stepped(step):
+        x = lax.rem(my_x + step[0], 4)
+        y = lax.rem(my_y + step[1], 4)
+        return lax.rem(x, 2) * 16 + y * 4 + (x // 2) * 2 + lax.rem(my_core + step[2], 2)
+
     barrier = pltpu.get_barrier_semaphore()
     for d in range(1, PLANES):
         pl.semaphore_signal(barrier, inc=1, device_id=z_peer(d), device_id_type=MESH)
@@ -305,8 +317,8 @@
     local = pltpu.make_async_copy(ret_send.at[my_p // 16], ret_buf.at[my_p], loc_sem.at[len(GROUPS)])
     local.start()
 
-    def send_back(i, carry):
-        peer = lax.rem(my_p + i, PEERS)
+    for step in STEPS:
+        peer = stepped(step)
         pltpu.make_async_remote_copy(
             src_ref=ret_send.at[peer // 16],
             dst_ref=ret_buf.at[my_p],
@@ -315,9 +327,6 @@
             device_id=p_peer(peer),
             device_id_type=MESH,
         ).start()
-        return carry
-
-    lax.fori_loop(1, PEERS, send_back, 0)
     number, lane = iota((16, 128), 0), iota((16, 128), 1)
     mine = jnp.where(
         number < 8,
@@ -353,7 +362,7 @@
             device_id_type=MESH,
         )
 
-    for d in range(1, PLANES):
+    for d in (4, 3, 5, 2, 6, 1, 7):
         z_back(d).start()
 
     upper = rel > 4

time: 55.1 us -> 54.7 us (level)
  no operation moved by 1% of the time
where the time goes in v4:
time: 54.7 us; the launch traced here: 54.6 us
  Pallas kernels  53.8 us (98%)
  local copies, waits for them, and re-layouts  0.57 us (1%)
    pallas_call x1, Pallas kernels, route(): pl.pallas_call(functools.partial(kernel, cap), out_shape=(jax.ShapeDtypeS...  53.8 us

profile of v4, /device:TPU:1, one launch (start us, length us, event | category | flops | bytes accessed | tf_op | source)
XLA Modules:
  0.0 54.6 jit_solution(17822568037700727188)
XLA Ops:
  0.0 0.0 copy-start
  0.0 53.8 %route_56.1 = (f32[1,256]{1,0:T(1,128)S(1)}, f32[1,128]{1,0:T(1,128)S(1)}, s32[1,256]{1,0:T(1,128)S(1)}, s32[1,256]{1,0:T(1,128)S(1)}) custom-call(bf16[256,1024]{1,0:T(8,128)(2,1)} %emb_hbm.1, s32[1,256]{1,0:T(1,128)} %bitcast.7, s32[1,256]{1,0:T(1,128)} %bitcast.8), custom_call_target="tpu_custom_call" | custom-call | tf_op jit(solution)/shard_map/route_56/pallas_call | solution.py:401
  53.8 0.0 copy-done
  53.8 0.2 conditional.1
  54.0 0.6 %copy.10 = f32[256]{0:T(256)} copy(f32[256]{0:T(256)S(1)} %get-tuple-element.29) | data formatting | bytes 2048
Async XLA Ops:
  0.0 53.8 %copy-start = (bf16[256,1024]{1,0:T(8,128)(2,1)S(1)}, bf16[256,1024]{1,0:T(8,128)(2,1)}, u32[]{:S(2)}) copy-start(bf16[256,1024]{1,0:T(8,128)(2,1)} %emb_hbm.1) | copy-start | bytes 1572868

commit v5 on v4

--- a/solution.py
+++ b/solution.py
@@ -14,7 +14,7 @@
 EMPTY = 2.0
 FAR = -8.0
 
-CAP = 56
+CAP = 52
 MOST = 128
 
 STEPS = sorted(
@@ -111,15 +111,13 @@
         return lax.rem(x, 2) * 16 + y * 4 + (x // 2) * 2 + lax.rem(my_core + step[2], 2)
 
     barrier = pltpu.get_barrier_semaphore()
-    for d in range(1, PLANES):
+    for d in (4, 3, 5, 2, 6, 1, 7):
         pl.semaphore_signal(barrier, inc=1, device_id=z_peer(d), device_id_type=MESH)
 
-    def greet(i, carry):
-        peer = lax.rem(my_p + i, PEERS)
-        pl.semaphore_signal(barrier, inc=1, device_id=p_peer(peer), device_id_type=MESH)
-        return carry
-
-    lax.fori_loop(1, PEERS, greet, 0)
+    for step in STEPS:
+        pl.semaphore_signal(
+            barrier, inc=1, device_id=p_peer(stepped(step)), device_id_type=MESH
+        )
 
     for load in loads[1:]:
         load.wait()
@@ -189,11 +187,11 @@
             slot[4 if d in (0, 4) else 8], pick, (((1,), (1,)), ((), ())), preferred_element_type=jnp.float32
         )[0:1, :]
         if d == 0:
-            zbuf[PLACE[d]] = rows
+            zbuf[PLACE[d]] = rows.reshape(cap // 4, 4, width)
             zmeta[d, :, 0:cap] = meta
             zmeta[d, :, 128:256] = jnp.broadcast_to(overflow, (1, 128))
         else:
-            zsend[d] = rows
+            zsend[d] = rows.reshape(cap // 4, 4, width)
             zmeta_send[d, :, 0:cap] = meta
             zmeta_send[d, :, 128:256] = jnp.broadcast_to(overflow, (1, 128))
             row_copy, meta_copy = z_copies(d)
@@ -412,9 +410,9 @@
             pltpu.VMEM((docs, width), jnp.bfloat16),
             pltpu.VMEM((1, docs), jnp.int32),
             pltpu.VMEM((1, docs), jnp.int32),
-            pltpu.VMEM((PLANES, cap, width), jnp.bfloat16),
+            pltpu.VMEM((PLANES, cap // 4, 4, width), jnp.bfloat16),
             pltpu.VMEM((PLANES, 1, 256), jnp.float32),
-            pltpu.VMEM((PLANES, cap, width), jnp.bfloat16),
+            pltpu.VMEM((PLANES, cap // 4, 4, width), jnp.bfloat16),
             pltpu.VMEM((PLANES, 1, 256), jnp.float32),
             [pltpu.VMEM((PEERS, n, width), jnp.bfloat16) for n in slots],
             [pltpu.VMEM((PEERS, n, width), jnp.bfloat16) for n in slots],

time: 54.7 us -> 53.5 us (0.978)
  Pallas kernels: 53.8 us -> 52.6 us
    pallas_call x1, Pallas kernels: 53.8 us -> 52.6 us  [route(): pl.pallas_call(functools.partial(kernel, cap), out_shape=(jax.ShapeDtypeS...]
where the time goes in v5:
time: 53.5 us; the launch traced here: 53.4 us
  Pallas kernels  52.6 us (98%)
  local copies, waits for them, and re-layouts  0.57 us (1%)
    pallas_call x1, Pallas kernels, route(): pl.pallas_call(functools.partial(kernel, cap), out_shape=(jax.ShapeDtypeS...  52.6 us

profile of v5, /device:TPU:1, one launch (start us, length us, event | category | flops | bytes accessed | tf_op | source)
XLA Modules:
  0.0 53.4 jit_solution(5908257866851488241)
XLA Ops:
  0.0 0.0 copy-start
  0.0 52.6 %route_52.1 = (f32[1,256]{1,0:T(1,128)S(1)}, f32[1,128]{1,0:T(1,128)S(1)}, s32[1,256]{1,0:T(1,128)S(1)}, s32[1,256]{1,0:T(1,128)S(1)}) custom-call(bf16[256,1024]{1,0:T(8,128)(2,1)} %emb_hbm.1, s32[1,256]{1,0:T(1,128)} %bitcast.7, s32[1,256]{1,0:T(1,128)} %bitcast.8), custom_call_target="tpu_custom_call" | custom-call | tf_op jit(solution)/shard_map/route_52/pallas_call | solution.py:399
  52.7 0.0 copy-done
  52.7 0.2 conditional.1
  52.9 0.6 %copy.10 = f32[256]{0:T(256)} copy(f32[256]{0:T(256)S(1)} %get-tuple-element.29) | data formatting | bytes 2048
Async XLA Ops:
  0.0 52.7 %copy-start = (bf16[256,1024]{1,0:T(8,128)(2,1)S(1)}, bf16[256,1024]{1,0:T(8,128)(2,1)}, u32[]{:S(2)}) copy-start(bf16[256,1024]{1,0:T(8,128)(2,1)} %emb_hbm.1) | copy-start | bytes 1572868

commit v6 on v5

--- a/solution.py
+++ b/solution.py
@@ -233,8 +233,7 @@
         local = pltpu.make_async_copy(psend.at[my_p], pbuf.at[my_p], loc_sem.at[g])
         local.start()
 
-        def send(i, carry):
-            peer = lax.rem(my_p + i, PEERS)
+        def send(peer):
             pltpu.make_async_remote_copy(
                 src_ref=psend.at[peer],
                 dst_ref=pbuf.at[my_p],
@@ -243,9 +242,16 @@
                 device_id=p_peer(peer),
                 device_id_type=MESH,
             ).start()
+
+        def send_next(i, carry):
+            send(lax.rem(my_p + i, PEERS))
             return carry
 
-        lax.fori_loop(1, PEERS, send, 0)
+        if g == len(GROUPS) - 1:
+            for step in STEPS:
+                send(stepped(step))
+        else:
+            lax.fori_loop(1, PEERS, send_next, 0)
         return functools.reduce(jnp.maximum, flags)
 
     def all_in_plane(src, dst, send_sem, recv_sem):
@@ -298,12 +304,11 @@
     for g in range(len(GROUPS)):
         if g == len(GROUPS) - 1:
             compare(0)
-            compare(1)
         if g == 2:
             for copy in z_copies(4):
                 copy.start()
         flag = jnp.maximum(flag, scatter(g))
-    for g in range(2, len(GROUPS)):
+    for g in range(1, len(GROUPS)):
         compare(g)
 
     ret_send[...] = jnp.zeros(ret_send.shape, jnp.float32)

time: 53.5 us -> 53.5 us (level)
  no operation moved by 1% of the time
where the time goes in v6:
time: 53.5 us
  Pallas kernels  52.6 us (98%)
  local copies, waits for them, and re-layouts  0.57 us (1%)
    pallas_call x1, Pallas kernels, route(): pl.pallas_call(functools.partial(kernel, cap), out_shape=(jax.ShapeDtypeS...  52.6 us

profile of v6, /device:TPU:1, one launch (start us, length us, event | category | flops | bytes accessed | tf_op | source)
XLA Modules:
  0.0 53.5 jit_solution(12349178168026668694)
XLA Ops:
  0.0 0.0 copy-start
  0.0 52.6 %route_52.1 = (f32[1,256]{1,0:T(1,128)S(1)}, f32[1,128]{1,0:T(1,128)S(1)}, s32[1,256]{1,0:T(1,128)S(1)}, s32[1,256]{1,0:T(1,128)S(1)}) custom-call(bf16[256,1024]{1,0:T(8,128)(2,1)} %emb_hbm.1, s32[1,256]{1,0:T(1,128)} %bitcast.7, s32[1,256]{1,0:T(1,128)} %bitcast.8), custom_call_target="tpu_custom_call" | custom-call | tf_op jit(solution)/shard_map/route_52/pallas_call | solution.py:404
  52.7 0.0 copy-done
  52.7 0.2 conditional.1
  52.9 0.6 %copy.10 = f32[256]{0:T(256)} copy(f32[256]{0:T(256)S(1)} %get-tuple-element.29) | data formatting | bytes 2048
Async XLA Ops:
  0.0 52.7 %copy-start = (bf16[256,1024]{1,0:T(8,128)(2,1)S(1)}, bf16[256,1024]{1,0:T(8,128)(2,1)}, u32[]{:S(2)}) copy-start(bf16[256,1024]{1,0:T(8,128)(2,1)} %emb_hbm.1) | copy-start | bytes 1572868
